TPU v7x, 32 devices: a whole 2x2x4 slice. The times are simulated.
32 devices in a mesh: slab: 4 (over y, x), brick: 8 (over z, core).
Axes of the slice: x: 2, y: 2, z: 4, core: 2. Of those that a mesh axis runs over, the one named last changes fastest.
Arguments:
- k_coeffs: float32 [8, 16, 16, 128], P('slab', 'brick'), may hold values from -0.3 to 0.4
- v_basis: float32 [32768, 128], P(('slab', 'brick')), may hold values from -4 to 4
Outputs:
- basis_x: float32 [8, 16, 16, 128], P('slab', 'brick')
- coupling: float32 [128, 128], replicated
- basis_v: float32 [32768, 128], P(('slab', 'brick'))
All inputs are finite; a program needn't handle non-finite values.
Results may differ from a plain program's by a relative error of at most 0.0001.
Values sent between devices are 32-bit elements; how exact they have to be, the bound alone decides.
A program may use at most 64 MiB of HBM per device.

v0:
```python
import math
import jax
import jax.numpy as jnp
from jax import lax
from jax.sharding import PartitionSpec as P

NVX = 32
CFL = 0.9
VMAX = 6.0
COLLIDE = 0.3
RHO_MIN = 0.25
TEMP_MIN = 0.25
PRECISE = lax.Precision.HIGHEST


def with_halo(array, sides, width):
    for axis, dim in sides:
        peers, length = (lax.axis_size(axis), array.shape[dim])
        up = [(i, (i + 1) % peers) for i in range(peers)]
        down = [(j, i) for i, j in up]
        last = lax.slice_in_dim(array, length - width, length, axis=dim)
        leading = lax.slice_in_dim(array, 0, width, axis=dim)
        before = lax.ppermute(last, axis, up)
        after = lax.ppermute(leading, axis, down)
        array = jnp.concatenate([before, array, after], axis=dim)
    return array


def velocities(indices):
    spacing = 2.0 * VMAX / NVX
    first_index = indices // (NVX * NVX)
    second = indices // NVX % NVX
    third_index = indices % NVX
    coords = jnp.stack([first_index, second, third_index]).astype(jnp.float32)
    return -VMAX + (coords + 0.5) * spacing


def maxwell(cell_params, velocity):
    distance = (velocity[0][None, :] - cell_params[1][:, None]) ** 2
    distance = distance + (velocity[1][None, :] - cell_params[2][:, None]) ** 2
    distance = distance + (velocity[2][None, :] - cell_params[3][:, None]) ** 2
    amplitude = cell_params[0] * (2.0 * math.pi * cell_params[4]) ** (-1.5)
    return amplitude[:, None] * jnp.exp(distance * (-0.5 / cell_params[4])[:, None])


def cell_state(vectors, coeffs):
    moments = lax.dot_general(vectors, coeffs, (((1,), (1,)), ((), ())), precision=PRECISE)
    density = jnp.maximum(moments[0], RHO_MIN)
    drift_speed = moments[1:4] / density[None, :]
    temper = jnp.maximum(
        (moments[4] / density - jnp.sum(drift_speed * drift_speed, axis=0)) / 3.0, TEMP_MIN
    )
    return jnp.concatenate([density[None], drift_speed, temper[None]], axis=0)


def transport_flux(backward, forward, transport):
    flux = jnp.zeros_like(backward[0])
    for axis_id in range(3):
        flux = flux + jnp.dot(backward[axis_id], transport[axis_id], precision=PRECISE)
        flux = flux + jnp.dot(forward[axis_id], transport[3 + axis_id], precision=PRECISE)
    return flux


def products(left_side, backward, forward, maxwell_proj):
    pieces = [
        lax.dot_general(left_side, item, (((0,), (0,)), ((), ())), precision=PRECISE)
        for item in backward + forward + [maxwell_proj]
    ]
    return jnp.stack(pieces)


def coupling_step(coupling_hat, minus_side, plus_side, projected, transport, time_step):
    drift_sum = jnp.zeros_like(coupling_hat)
    for axis_id in range(3):
        drift_sum = drift_sum + jnp.dot(
            jnp.dot(minus_side[axis_id], coupling_hat, precision=PRECISE),
            transport[axis_id],
            precision=PRECISE,
        )
        drift_sum = drift_sum + jnp.dot(
            jnp.dot(plus_side[axis_id], coupling_hat, precision=PRECISE),
            transport[3 + axis_id],
            precision=PRECISE,
        )
    return coupling_hat + time_step * drift_sum - COLLIDE * (projected - coupling_hat)


def velocity_step(velocity_part, minus_side, plus_side, back_proj, positive, negative, time_step):
    drift_sum = jnp.zeros_like(velocity_part)
    for axis_id in range(3):
        drift_sum = drift_sum + positive[axis_id][:, None] * jnp.dot(
            velocity_part, minus_side[axis_id].T, precision=PRECISE
        )
        drift_sum = drift_sum + negative[axis_id][:, None] * jnp.dot(
            velocity_part, plus_side[axis_id].T, precision=PRECISE
        )
    return velocity_part - time_step * drift_sum + COLLIDE * (back_proj - velocity_part)


def slopes(padded, lengths):
    rank_size = padded.shape[3]
    centre = padded[1:-1, 1:-1]
    backward = [
        (centre - padded[:-2, 1:-1]) * lengths[0],
        (centre - padded[1:-1, :-2]) * lengths[1],
        (centre - jnp.roll(centre, 1, axis=2)) * lengths[2],
    ]
    forward = [
        (padded[2:, 1:-1] - centre) * lengths[0],
        (padded[1:-1, 2:] - centre) * lengths[1],
        (jnp.roll(centre, -1, axis=2) - centre) * lengths[2],
    ]
    return (
        [item.reshape(-1, rank_size) for item in backward],
        [item.reshape(-1, rank_size) for item in forward],
    )


def local(k_coeffs, v_basis):
    cells_x, cells_y, cells_z, rank_size = k_coeffs.shape
    cell_count = cells_x * cells_y * cells_z
    slab_count = lax.axis_size("slab")
    brick_count = lax.axis_size("brick")
    devices = slab_count * brick_count
    lengths = (cells_x * slab_count, cells_y * brick_count, cells_z)
    time_step = CFL / (VMAX * (lengths[0] + lengths[1] + lengths[2]))
    weight_x = 1.0 / (lengths[0] * lengths[1] * lengths[2])
    weight_v = (2.0 * VMAX / NVX) ** 3
    row_count = v_basis.shape[0]
    device = lax.axis_index("slab") * brick_count + lax.axis_index("brick")
    row_ids = device * row_count + jnp.arange(row_count, dtype=jnp.int32)
    velocity = velocities(row_ids)
    positive = jnp.maximum(velocity, 0.0)
    negative = jnp.minimum(velocity, 0.0)
    weights = jnp.stack(
        [
            jnp.ones_like(velocity[0]),
            velocity[0],
            velocity[1],
            velocity[2],
            jnp.sum(velocity * velocity, axis=0),
        ]
    )
    vectors = jnp.dot(weights, v_basis, precision=PRECISE) * weight_v
    transport = jnp.stack(
        [
            lax.dot_general(
                v_basis * (side[axis_id] * weight_v)[:, None],
                v_basis,
                (((0,), (0,)), ((), ())),
                precision=PRECISE,
            )
            for side in (positive, negative)
            for axis_id in range(3)
        ]
    )
    transport, vectors = lax.psum((transport, vectors), ("slab", "brick"))
    coeff_flat = k_coeffs.reshape(cell_count, rank_size)
    cell_params = cell_state(vectors, coeff_flat)
    params_all = lax.all_gather(cell_params, ("slab", "brick"), axis=1, tiled=True)
    row_total = cell_count * devices
    block_rows = math.gcd(row_total, 512)

    def one_block(turn_index):
        part_params = lax.dynamic_slice_in_dim(
            params_all, 0 + turn_index * block_rows, block_rows, 1
        )
        return jnp.dot(maxwell(part_params, velocity), v_basis, precision=PRECISE) * weight_v

    blocks = lax.map(one_block, jnp.arange(row_total // block_rows, dtype=jnp.int32))
    whole_term = lax.psum(blocks.reshape(row_total, rank_size), ("slab", "brick"))
    maxwell_proj = lax.dynamic_slice_in_dim(whole_term, device * cell_count, cell_count, 0)
    padded = with_halo(k_coeffs, (("slab", 0), ("brick", 1)), 1)
    backward, forward = slopes(padded, lengths)
    advanced = (
        coeff_flat
        - time_step * transport_flux(backward, forward, transport)
        + COLLIDE * (maxwell_proj - coeff_flat)
    )
    identity = jnp.eye(rank_size, dtype=jnp.float32)
    padded_new = with_halo(
        advanced.reshape(cells_x, cells_y, cells_z, rank_size), (("slab", 0), ("brick", 1)), 1
    )
    backward, forward = slopes(padded_new, lengths)
    local_sums = jnp.concatenate(
        [
            lax.dot_general(advanced, advanced, (((0,), (0,)), ((), ())), precision=PRECISE)[None],
            products(advanced, backward, forward, maxwell_proj),
        ],
        axis=0,
    )
    reduced_all = lax.psum(local_sums * weight_x, ("slab", "brick"))
    factor = jnp.linalg.cholesky(reduced_all[0])
    inverse = jax.scipy.linalg.solve_triangular(factor, identity, lower=True)
    basis_new = jnp.dot(advanced, inverse.T, precision=PRECISE)
    mapped = jnp.einsum("ab,kbc,dc->kad", inverse, reduced_all[1:7], inverse, precision=PRECISE)
    minus_side = mapped[0:3]
    plus_side = mapped[3:6]
    projected = jnp.dot(inverse, reduced_all[7], precision=PRECISE)
    coupling_mid = coupling_step(factor.T, minus_side, plus_side, projected, transport, time_step)
    rows_piece = lax.all_gather(basis_new, ("slab", "brick"), axis=0, tiled=True)
    piece_rows = rows_piece.shape[0]
    fold_block_rows = math.gcd(piece_rows, 512)

    def add_block(turn_index, accumulated):
        offset = turn_index * fold_block_rows
        part_params = lax.dynamic_slice_in_dim(params_all, offset, fold_block_rows, 1)
        basis_block = lax.dynamic_slice_in_dim(rows_piece, offset, fold_block_rows, 0)
        values = maxwell(part_params, velocity)
        return (
            accumulated
            + lax.dot_general(values, basis_block, (((0,), (0,)), ((), ())), precision=PRECISE)
            * weight_x
        )

    back_proj = lax.fori_loop(
        0, piece_rows // fold_block_rows, add_block, jnp.zeros((row_count, rank_size), jnp.float32)
    )
    velocity_part = jnp.dot(v_basis, coupling_mid.T, precision=PRECISE)
    velocity_new = velocity_step(
        velocity_part, minus_side, plus_side, back_proj, positive, negative, time_step
    )
    gram_v = (
        lax.dot_general(velocity_new, velocity_new, (((0,), (0,)), ((), ())), precision=PRECISE)
        * weight_v
    )
    gram_v = lax.psum(gram_v, ("slab", "brick"))
    coupling = jnp.linalg.cholesky(gram_v)
    inverse_v = jax.scipy.linalg.solve_triangular(coupling, identity, lower=True)
    vbasis_new = jnp.dot(velocity_new, inverse_v.T, precision=PRECISE)
    return (basis_new.reshape(cells_x, cells_y, cells_z, rank_size), coupling, vbasis_new)


def solution(mesh):
    placed = (P("slab", "brick", None, None), P(("slab", "brick"), None))
    return jax.shard_map(
        local,
        mesh=mesh,
        in_specs=placed,
        out_specs=(P("slab", "brick", None, None), P(), P(("slab", "brick"), None)),
        check_vma=False,
    )
```

profile of v0, /device:TPU:1, one launch (start us, length us, event | category | flops | bytes accessed | tf_op | source)
XLA Modules:
  0.0 666.3 jit_solution(5660774620069274221)
XLA Ops:
  8.0 2.0 collective-permute-start
  10.0 1.0 collective-permute-start.1
  11.1 1.4 convolution_multiply_fusion.7
  12.6 39.6 %psum.36 = f32[5,128]{1,0:T(8,128)S(1)} all-reduce(f32[5,128]{1,0:T(8,128)S(1)} %convolution_multiply_fusion.7), channel_id=1, replica_groups=mesh['slab'=4,'brick'=8] {'slab','brick'}, use_global_device_ids=true, to_apply=%region_2.3 | all-reduce | flops 640 | bytes 5120 | tf_op jit(solution)/shard_map/psum | solution.py:157
  53.1 43.0 %all-gather = f32[32,64,5]{1,2,0:T(8,128)S(1)} all-gather(f32[1,64,5]{1,2,0:T(8,128)S(1)} %maximum_bitcast_fusion), channel_id=1, replica_groups=mesh['slab'=4,'brick'=8] {'slab','brick'}, dimensions={0}, use_global_device_ids=true | all-gather | bytes 42240 | tf_op jit(solution)/shard_map/all_gather | solution.py:160
  96.2 18.5 %while.24 = (s32[]{:T(128)}, f32[4,512,128]{2,1,0:T(8,128)}, s32[4]{0:T(128)S(1)}, f32[5,2048]{1,0:T(8,128)S(1)}, f32[3,1024]{1,0:T(4,128)S(1)}, /*index=5*/f32[...) while((s32[]{:T(128)}, f32[4,512,128]{2,1,0:T(8,128)}, ...), condition=%wide.region_5.6_spmd, body=%wide.region_4.5_spmd.sunk | while | flops 810616320 | bytes 854787 | solution.py:170
  97.6 3.3 fusion.244
  102.2 3.3 fusion.244
  106.8 3.3 fusion.244
  111.5 3.3 fusion.244
  114.8 1.2 fusion.82
  116.0 1.2 fusion.81
  117.2 1.2 fusion.80
  118.3 1.2 fusion.79
  119.5 1.2 fusion.78
  120.7 1.2 fusion.77
  122.8 0.9 collective-permute-start.3
  124.0 3.9 collective-permute-done.3
  128.0 122.3 %all-reduce.9.cloned.1.call-done = (f32[6,128,128]{2,1,0:T(8,128)}, f32[2048,128]{1,0:T(8,128)}) async-done(((f32[6,128,128]{2,1,0:T(8,128)}, f32[2048,128]{1,0:T(8,128)}), (f32[6,128,128]{2,1,0:T(8,128)}, f32[2048,128]{1,0:T(8,128)})) %all-reduce.9.cloned.1.call-update) | async-done | bytes 1441808 | tf_op jit(solution)/shard_map/psum | solution.py:157
  250.3 1.0 fusion.113
  251.4 1.0 convolution_add_fusion.9
  252.4 1.0 convolution_add_fusion.8
  253.4 1.0 convolution_add_fusion.7
  254.5 1.0 convolution_add_fusion.6
  255.5 1.0 fusion.85
  256.6 1.2 collective-permute-start.4
  257.8 1.2 collective-permute-start.5
  259.0 1.1 collective-permute-done.4
  260.4 4.1 collective-permute-start.6
  265.6 2.7 collective-permute-done.7
  270.1 1.1 fusion.69
  272.1 129.2 %all-reduce.5.cloned.1.call-done = f32[8,128,128]{1,2,0:T(8,128)} async-done(((f32[8,128,128]{1,2,0:T(8,128)}), f32[8,128,128]{1,2,0:T(8,128)}) %all-reduce.5.cloned.1.call-update) | async-done | bytes 524304 | tf_op jit(solution)/shard_map/psum | solution.py:192
  403.2 11.7 %cholesky.44 = f32[128,128]{1,0:T(8,128)S(1)} custom-call(f32[128,128]{1,0:T(8,128)S(1)} %fusion.103), custom_call_target="Cholesky" | custom-call | tf_op jit(solution)/shard_map/jit(cholesky)/cholesky | solution.py:193
  416.2 9.8 %custom-call.7 = f32[1,128,128]{1,2,0:T(8,128)S(1)} custom-call(f32[1,128,128]{2,1,0:T(8,128)S(1)} %select_bitcast_fusion.1), custom_call_target="InvertDiagBlocksLowerTriangular" | custom-call | tf_op jit(solution)/shard_map/jit(_solve_triangular)/triangular_solve | solution.py:194
  435.4 0.9 fusion.68
  441.0 47.2 %all-gather.3.cloned.1.call-done = f32[2048,128]{1,0:T(8,128)} async-done(((f32[64,128]{1,0:T(8,128)}), f32[2048,128]{1,0:T(8,128)}) %all-gather.3.cloned.1.call-update) | async-done | bytes 1048592 | tf_op jit(solution)/shard_map/all_gather | solution.py:201
  488.2 21.7 %while.25 = (s32[]{:T(128)}, f32[1024,128]{1,0:T(8,128)S(1)}, f32[5,2048]{1,0:T(8,128)S(1)}, f32[3,1024]{1,0:T(4,128)S(1)}, f32[2048,128]{1,0:T(8,128)}, /*index...) while((s32[]{:T(128)}, f32[1024,128]{1,0:T(8,128)S(1)}, ...), condition=%wide.region_11.14_spmd.clone, body=%wide.region_10.13_spmd.clone.sunk | while | flops 810944000 | bytes 1378557 | solution.py:216
  488.3 5.2 fusion.248
  493.7 5.2 fusion.248
  499.1 5.2 fusion.248
  504.5 5.2 fusion.248
  510.9 1.2 convolution_multiply_fusion.6
  512.1 120.0 %all-reduce.7.cloned.1.call-done = f32[128,128]{0,1:T(8,128)} async-done(((f32[128,128]{0,1:T(8,128)}), f32[128,128]{0,1:T(8,128)}) %all-reduce.7.cloned.1.call-update) | async-done | bytes 65552 | tf_op jit(solution)/shard_map/psum | solution.py:227
  632.2 0.9 copy.68
  633.9 11.7 %cholesky.55 = f32[128,128]{1,0:T(8,128)S(1)} custom-call(f32[128,128]{1,0:T(8,128)S(1)} %fusion.105), custom_call_target="Cholesky" | custom-call | tf_op jit(solution)/shard_map/jit(cholesky)/cholesky | solution.py:228
  646.3 1.3 select_bitcast_fusion
  647.6 9.8 %custom-call.8 = f32[1,128,128]{1,2,0:T(8,128)S(1)} custom-call(f32[1,128,128]{2,1,0:T(8,128)S(1)} %get-tuple-element.175), custom_call_target="InvertDiagBlocksLowerTriangular" | custom-call | tf_op jit(solution)/shard_map/jit(_solve_triangular)/triangular_solve | solution.py:229
  657.7 1.8 fusion.178
  (126 shorter events, 30.3 us)
Async XLA Ops:
  7.2 89.0 %copy-start = (f32[1024,128]{1,0:T(8,128)S(1)}, f32[1024,128]{1,0:T(8,128)}, u32[]{:S(2)}) copy-start(f32[1024,128]{1,0:T(8,128)} %param.10) | copy-start | bytes 1572868
  7.2 243.2 %all-reduce.9.cloned.1.call-start = ((), (), s32[]{:S(2)}) async-start(), calls=%async_computation.3 | async-start | bytes 2883584 | tf_op jit(solution)/shard_map/psum | solution.py:157
  8.0 114.7 %collective-permute-start = (f32[1,2,16,128]{3,2,1,0:T(8,128)S(1)}, f32[1,2,16,128]{3,2,1,0:T(8,128)S(1)}, u32[]{:S(2)}, u32[]{:S(2)}) collective-permute-start(f32[1,2,16,128]{3,2,1,0:T(8,128)S(1)} %get-tuple-element.222), channel_id=1, source_target_pairs={{0,8},{8,16},{16,24},{24,0},{1,9},{9,17},{17,25},{25,1},{2,10},{10... | collective-permute-start | bytes 49160 | tf_op jit(solution)/shard_map/ppermute | solution.py:23
  10.0 112.7 %collective-permute-start.1 = (f32[1,2,16,128]{3,2,1,0:T(8,128)S(1)}, f32[1,2,16,128]{3,2,1,0:T(8,128)S(1)}, u32[]{:S(2)}, u32[]{:S(2)}) collective-permute-start(f32[1,2,16,128]{3,2,1,0:T(8,128)S(1)} %get-tuple-element.221), channel_id=1, source_target_pairs={{8,0},{16,8},{24,16},{0,24},{9,1},{17,9},{25,17},{1,25},{10,2},{18... | collective-permute-start | bytes 49160 | tf_op jit(solution)/shard_map/ppermute | solution.py:24
  120.7 2.0 copy-start.1
  121.9 0.7 copy-start.4
  122.6 278.7 %all-reduce.5.cloned.1.call-start = ((), (), s32[]{:S(2)}) async-start(), calls=%async_computation | async-start | bytes 1048576 | tf_op jit(solution)/shard_map/psum | solution.py:192
  122.8 1.3 collective-permute-start.2
  122.8 5.1 collective-permute-start.3
  256.6 3.5 collective-permute-start.4
  257.8 2.6 collective-permute-start.5
  260.4 5.1 collective-permute-start.6
  264.5 3.8 collective-permute-start.7
  272.0 216.2 %all-gather.3.cloned.1.call-start = ((), (), s32[]{:S(2)}) async-start(), calls=%async_computation.1 | async-start | bytes 1081344 | tf_op jit(solution)/shard_map/all_gather | solution.py:201
  401.3 25.0 %copy-start.3 = (f32[8,128,128]{1,2,0:T(8,128)S(1)}, f32[8,128,128]{1,2,0:T(8,128)}, u32[]{:S(2)}) copy-start(f32[8,128,128]{1,2,0:T(8,128)} %all-reduce.5.cloned.1.call-done) | copy-start | bytes 1572868
  426.8 6.9 %copy-start.2 = (f32[6,128,128]{2,1,0:T(8,128)S(1)}, f32[6,128,128]{2,1,0:T(8,128)}, u32[]{:S(2)}) copy-start(f32[6,128,128]{2,1,0:T(8,128)} %get-tuple-element.173) | copy-start | bytes 1179652
  434.0 198.1 %all-reduce.7.cloned.1.call-start = ((), (), s32[]{:S(2)}) async-start(), calls=%async_computation.2 | async-start | bytes 131072 | tf_op jit(solution)/shard_map/psum | solution.py:227
Sparse Core Ops, SparseCore 0:
  122.8 127.5 all-reduce.8
  272.1 129.1 all-reduce.4
  434.1 54.0 all-gather.2
  512.3 119.8 all-reduce.6
where the time goes:
time: 676 us; the launch traced here: 666 us
  waiting for transfers between devices  428 us (63%)
  blocking collectives  82.5 us (12%)
  matrix products  71.2 us (11%)
  other arithmetic  49.9 us (7%)
  between operations  14.6 us (2%)
  starting transfers between devices  10.9 us (2%)
    psum x1, waiting for transfers between devices, local(): reduced_all = lax.psum(local_sums * weight_x, ('slab', 'brick'))  129 us
    psum x1, waiting for transfers between devices, local(): transport, vectors = lax.psum((transport, vectors), ('slab', 'brick'))  122 us
    psum x1, waiting for transfers between devices, local(): gram_v = lax.psum(gram_v, ('slab', 'brick'))  120 us
    all_gather x1, waiting for transfers between devices, local(): lax.all_gather(basis_new, ('slab', 'brick'), axis=0, tiled=True)  47.2 us
    all_gather x1, blocking collectives, local(): lax.all_gather(cell_params, ('slab', 'brick'), axis=1, tiled=True)  43 us
    psum x1, blocking collectives, local(): transport, vectors = lax.psum((transport, vectors), ('slab', 'brick'))  39.6 us
    dot_general x4, matrix products, add_block(): lax.dot_general(values, basis_block, (((0,), (0,)), ((), ())), precision=...  21 us
  transfers between devices with their start and end apart: 12, of which 10 were waited for; matrix products, arithmetic and copies ran while one was open for 5% of the time, Pallas kernels for 0%

commit v1 on v0

--- a/solution.py
+++ b/solution.py
@@ -224,7 +224,7 @@
         lax.dot_general(velocity_new, velocity_new, (((0,), (0,)), ((), ())), precision=PRECISE)
         * weight_v
     )
-    gram_v = lax.psum(gram_v, ("slab", "brick"))
+    gram_v = jnp.sum(lax.all_gather(gram_v, ("slab", "brick")), axis=0)
     coupling = jnp.linalg.cholesky(gram_v)
     inverse_v = jax.scipy.linalg.solve_triangular(coupling, identity, lower=True)
     vbasis_new = jnp.dot(velocity_new, inverse_v.T, precision=PRECISE)

time: 676 us -> 619 us (0.916)
  waiting for transfers between devices: 428 us -> 363 us
  matrix products: 71.2 us -> 79.8 us
    psum x1 -> x0, waiting for transfers between devices: 120 us -> none  [local(): gram_v = lax.psum(gram_v, ('slab', 'brick'))]
    all_gather x0 -> x1, waiting for transfers between devices: none -> 55.5 us  [local(): gram_v = jnp.sum(lax.all_gather(gram_v, ('slab', 'brick')), axis=0)]
  transfers between devices with their start and end apart: 12 -> 12, of which waited for: 10 -> 10; matrix products, arithmetic and copies ran while one was open for 5% -> 7% of each run, Pallas kernels for 0% -> 0%
where the time goes in v1:
time: 619 us; the launch traced here: 609 us
  waiting for transfers between devices  363 us (59%)
  blocking collectives  82.5 us (13%)
  matrix products  79.8 us (13%)
  other arithmetic  50.8 us (8%)
  between operations  14.6 us (2%)
  starting transfers between devices  10.9 us (2%)
    psum x1, waiting for transfers between devices, local(): reduced_all = lax.psum(local_sums * weight_x, ('slab', 'brick'))  129 us
    psum x1, waiting for transfers between devices, local(): transport, vectors = lax.psum((transport, vectors), ('slab', 'brick'))  122 us
    all_gather x1, waiting for transfers between devices, local(): gram_v = jnp.sum(lax.all_gather(gram_v, ('slab', 'brick')), axis=0)  55.5 us
    all_gather x1, waiting for transfers between devices, local(): lax.all_gather(basis_new, ('slab', 'brick'), axis=0, tiled=True)  46.3 us
    all_gather x1, blocking collectives, local(): lax.all_gather(cell_params, ('slab', 'brick'), axis=1, tiled=True)  43 us
    psum x1, blocking collectives, local(): transport, vectors = lax.psum((transport, vectors), ('slab', 'brick'))  39.6 us
    dot_general x4, matrix products, add_block(): lax.dot_general(values, basis_block, (((0,), (0,)), ((), ())), precision=...  21 us
    dot_general x4, matrix products, one_block(): jnp.dot(maxwell(part_params, velocity), v_basis, precision=PRECISE)  17.3 us
  transfers between devices with their start and end apart: 12, of which 10 were waited for; matrix products, arithmetic and copies ran while one was open for 7% of the time, Pallas kernels for 0%

profile of v1, /device:TPU:1, one launch (start us, length us, event | category | flops | bytes accessed | tf_op | source)
XLA Modules:
  0.0 609.4 jit_solution(7442161873554444593)
XLA Ops:
  7.9 2.0 collective-permute-start
  10.0 1.0 collective-permute-start.1
  11.1 1.4 convolution_multiply_fusion.7
  12.5 39.6 %psum.29 = f32[5,128]{1,0:T(8,128)S(1)} all-reduce(f32[5,128]{1,0:T(8,128)S(1)} %convolution_multiply_fusion.7), channel_id=1, replica_groups=mesh['slab'=4,'brick'=8] {'slab','brick'}, use_global_device_ids=true, to_apply=%region_2.3 | all-reduce | flops 640 | bytes 5120 | tf_op jit(solution)/shard_map/psum | solution.py:157
  53.1 43.0 %all-gather.1 = f32[32,64,5]{1,2,0:T(8,128)S(1)} all-gather(f32[1,64,5]{1,2,0:T(8,128)S(1)} %maximum_bitcast_fusion), channel_id=1, replica_groups=mesh['slab'=4,'brick'=8] {'slab','brick'}, dimensions={0}, use_global_device_ids=true | all-gather | bytes 42240 | tf_op jit(solution)/shard_map/all_gather | solution.py:160
  96.1 22.7 %while.24 = (s32[]{:T(128)}, f32[4,512,128]{2,1,0:T(8,128)}, s32[4]{0:T(128)S(1)}, f32[5,2048]{1,0:T(8,128)S(1)}, f32[3,1024]{1,0:T(4,128)S(1)}, /*index=5*/f32[...) while((s32[]{:T(128)}, f32[4,512,128]{2,1,0:T(8,128)}, ...), condition=%wide.region_5.6_spmd, body=%wide.region_4.5_spmd.sunk | while | flops 810616320 | bytes 854787 | solution.py:170
  97.5 4.3 fusion.244
  103.2 4.3 fusion.244
  108.9 4.3 fusion.244
  114.5 4.3 fusion.244
  118.9 2.4 fusion.82
  121.4 2.4 fusion.81
  123.8 1.2 fusion.80
  125.0 1.2 fusion.79
  126.2 1.2 fusion.78
  127.4 1.2 fusion.77
  130.7 3.9 collective-permute-done.3
  134.7 122.4 %all-reduce.6.cloned.1.call-done = (f32[6,128,128]{2,1,0:T(8,128)}, f32[2048,128]{1,0:T(8,128)}) async-done(((f32[6,128,128]{2,1,0:T(8,128)}, f32[2048,128]{1,0:T(8,128)}), (f32[6,128,128]{2,1,0:T(8,128)}, f32[2048,128]{1,0:T(8,128)})) %all-reduce.6.cloned.1.call-update) | async-done | bytes 1441808 | tf_op jit(solution)/shard_map/psum | solution.py:157
  257.0 1.0 fusion.113
  258.1 1.0 convolution_add_fusion.9
  259.1 1.0 convolution_add_fusion.8
  260.1 1.0 convolution_add_fusion.7
  261.1 1.0 convolution_add_fusion.6
  262.2 1.0 fusion.85
  263.3 1.2 collective-permute-start.4
  264.5 1.2 collective-permute-start.5
  265.7 1.1 collective-permute-done.4
  267.1 4.1 collective-permute-start.6
  272.3 2.7 collective-permute-done.7
  276.8 1.1 fusion.69
  278.8 129.2 %all-reduce.4.cloned.1.call-done = f32[8,128,128]{1,2,0:T(8,128)} async-done(((f32[8,128,128]{1,2,0:T(8,128)}), f32[8,128,128]{1,2,0:T(8,128)}) %all-reduce.4.cloned.1.call-update) | async-done | bytes 524304 | tf_op jit(solution)/shard_map/psum | solution.py:192
  409.8 11.7 %cholesky.44 = f32[128,128]{1,0:T(8,128)S(1)} custom-call(f32[128,128]{1,0:T(8,128)S(1)} %fusion.103), custom_call_target="Cholesky" | custom-call | tf_op jit(solution)/shard_map/jit(cholesky)/cholesky | solution.py:193
  422.9 9.8 %custom-call.7 = f32[1,128,128]{1,2,0:T(8,128)S(1)} custom-call(f32[1,128,128]{2,1,0:T(8,128)S(1)} %select_bitcast_fusion.1), custom_call_target="InvertDiagBlocksLowerTriangular" | custom-call | tf_op jit(solution)/shard_map/jit(_solve_triangular)/triangular_solve | solution.py:194
  433.0 1.5 fusion.108
  444.0 1.8 fusion.66
  449.5 46.3 %all-gather.5.cloned.1.call-done = f32[2048,128]{1,0:T(8,128)} async-done(((f32[64,128]{1,0:T(8,128)}), f32[2048,128]{1,0:T(8,128)}) %all-gather.5.cloned.1.call-update) | async-done | bytes 1048592 | tf_op jit(solution)/shard_map/all_gather | solution.py:201
  495.9 21.7 %while.25 = (s32[]{:T(128)}, f32[1024,128]{1,0:T(8,128)S(1)}, f32[5,2048]{1,0:T(8,128)S(1)}, f32[3,1024]{1,0:T(4,128)S(1)}, f32[2048,128]{1,0:T(8,128)}, /*index...) while((s32[]{:T(128)}, f32[1024,128]{1,0:T(8,128)S(1)}, ...), condition=%wide.region_11.14_spmd.clone, body=%wide.region_10.13_spmd.clone.sunk | while | flops 810944000 | bytes 1378557 | solution.py:216
  496.0 5.2 fusion.248
  501.4 5.2 fusion.248
  506.7 5.2 fusion.248
  512.1 5.2 fusion.248
  518.5 1.2 convolution_multiply_fusion.6
  519.8 55.5 %all-gather.7.cloned.1.call-done = f32[4096,128]{1,0:T(8,128)} async-done(((f32[128,128]{1,0:T(8,128)}), f32[4096,128]{1,0:T(8,128)}) %all-gather.7.cloned.1.call-update) | async-done | bytes 2097168 | tf_op jit(solution)/shard_map/all_gather | solution.py:227
  575.3 1.7 reduce_sum.32
  577.1 11.7 %cholesky.55 = f32[128,128]{1,0:T(8,128)S(1)} custom-call(f32[128,128]{1,0:T(8,128)S(1)} %fusion.105), custom_call_target="Cholesky" | custom-call | tf_op jit(solution)/shard_map/jit(cholesky)/cholesky | solution.py:228
  589.5 1.3 select_bitcast_fusion
  590.8 9.8 %custom-call.8 = f32[1,128,128]{1,2,0:T(8,128)S(1)} custom-call(f32[1,128,128]{2,1,0:T(8,128)S(1)} %get-tuple-element.175), custom_call_target="InvertDiagBlocksLowerTriangular" | custom-call | tf_op jit(solution)/shard_map/jit(_solve_triangular)/triangular_solve | solution.py:229
  600.9 1.8 fusion.178
  (125 shorter events, 29.8 us)
Async XLA Ops:
  7.2 249.9 %all-reduce.6.cloned.1.call-start = ((), (), s32[]{:S(2)}) async-start(), calls=%async_computation.3 | async-start | bytes 2883584 | tf_op jit(solution)/shard_map/psum | solution.py:157
  7.9 121.4 %collective-permute-start = (f32[1,2,16,128]{3,2,1,0:T(8,128)S(1)}, f32[1,2,16,128]{3,2,1,0:T(8,128)S(1)}, u32[]{:S(2)}, u32[]{:S(2)}) collective-permute-start(f32[1,2,16,128]{3,2,1,0:T(8,128)S(1)} %get-tuple-element.222), channel_id=1, source_target_pairs={{0,8},{8,16},{16,24},{24,0},{1,9},{9,17},{17,25},{25,1},{2,10},{10... | collective-permute-start | bytes 49160 | tf_op jit(solution)/shard_map/ppermute | solution.py:23
  10.0 119.4 %collective-permute-start.1 = (f32[1,2,16,128]{3,2,1,0:T(8,128)S(1)}, f32[1,2,16,128]{3,2,1,0:T(8,128)S(1)}, u32[]{:S(2)}, u32[]{:S(2)}) collective-permute-start(f32[1,2,16,128]{3,2,1,0:T(8,128)S(1)} %get-tuple-element.221), channel_id=1, source_target_pairs={{8,0},{16,8},{24,16},{0,24},{9,1},{17,9},{25,17},{1,25},{10,2},{18... | collective-permute-start | bytes 49160 | tf_op jit(solution)/shard_map/ppermute | solution.py:24
  118.9 4.9 copy-start
  126.2 3.2 copy-start.1
  128.5 0.7 copy-start.3
  129.3 278.7 %all-reduce.4.cloned.1.call-start = ((), (), s32[]{:S(2)}) async-start(), calls=%async_computation | async-start | bytes 1048576 | tf_op jit(solution)/shard_map/psum | solution.py:192
  129.5 1.3 collective-permute-start.2
  129.5 5.1 collective-permute-start.3
  263.3 3.5 collective-permute-start.4
  264.5 2.6 collective-permute-start.5
  267.1 5.1 collective-permute-start.6
  271.2 3.8 collective-permute-start.7
  278.7 162.6 %copy-start.2 = (f32[6,128,128]{2,1,0:T(8,128)S(1)}, f32[6,128,128]{2,1,0:T(8,128)}, u32[]{:S(2)}) copy-start(f32[6,128,128]{2,1,0:T(8,128)} %get-tuple-element.173) | copy-start | bytes 1179652
  278.7 217.1 %all-gather.5.cloned.1.call-start = ((), (), s32[]{:S(2)}) async-start(), calls=%async_computation.1 | async-start | bytes 1081344 | tf_op jit(solution)/shard_map/all_gather | solution.py:201
  441.6 133.6 %all-gather.7.cloned.1.call-start = ((), (), s32[]{:S(2)}) async-start(), calls=%async_computation.2 | async-start | bytes 2162688 | tf_op jit(solution)/shard_map/all_gather | solution.py:227
Sparse Core Ops, SparseCore 0:
  129.4 127.5 all-reduce.5
  278.8 129.1 all-reduce.3
  441.8 54.0 all-gather.4
  519.9 55.3 all-gather.6
